TPU v7x, 256 devices: a whole 4x4x8 slice. The times are simulated.
256 devices in a mesh: req: 8 (over y_hi, x), blk: 32 (over y_lo, z, core).
Axes of the slice: x: 4, y: 4 (y_hi: 2, y_lo: 2; y = y_hi * 2 + y_lo), z: 8, core: 2. Of those that a mesh axis runs over, the one named last changes fastest.
Arguments:
- prefill_resid: bfloat16 [1024, 2048], P(('blk', 'req')), may hold values from -3 to 3
- prefill_routes: int32 [1024, 6], P(('blk', 'req')), may hold values from 0 to 63, all different within a row; in each aligned block of 32 rows (0 to 31, 32 to 63, ...) at most 6 rows name the same one
- prefill_scores: float32 [1024, 6], P(('blk', 'req')), may hold values from 0.05 to 1
- decode_resid: bfloat16 [16, 2048], P('req'), may hold values from -3 to 3
- queries: bfloat16 [16, 16, 192], P('req'), may hold values from -8 to 8
- latent_cache: bfloat16 [16, 16384, 576], P('req', 'blk'), may hold values from -8 to 8
- new_latent: bfloat16 [16, 576], P('req'), may hold values from -8 to 8
- cache_lengths: int32 [16], P('req'), may hold values from 1 to 16384, 65536 in all
- decode_routes: int32 [16, 6], P('req'), may hold values from 0 to 63, all different within a row
- decode_scores: float32 [16, 6], P('req'), may hold values from 0.05 to 1
- norm_gain: float32 [2048], replicated, may hold values from 0.1 to 1.9
- absorb_key: bfloat16 [16, 128, 512], replicated, may hold values from -0.5 to 0.5
- absorb_value: bfloat16 [16, 512, 128], P('req'), may hold values from -6 to 6
- out_proj: bfloat16 [16, 128, 2048], P('req'), may hold values from -0.125 to 0.125
- expert_gate: bfloat16 [64, 2048, 1408], P('blk', None, 'req'), may hold values from -0.125 to 0.125
- expert_up: bfloat16 [64, 2048, 1408], P('blk', None, 'req'), may hold values from -0.125 to 0.125
- expert_down: bfloat16 [64, 1408, 2048], P('blk', 'req'), may hold values from -0.15625 to 0.15625
- shared_gate: bfloat16 [2048, 2816], P(None, 'req'), may hold values from -0.125 to 0.125
- shared_up: bfloat16 [2048, 2816], P(None, 'req'), may hold values from -0.125 to 0.125
- shared_down: bfloat16 [2816, 2048], P('req'), may hold values from -0.109375 to 0.109375
Outputs:
- prefill_out: bfloat16 [1024, 2048], P(('blk', 'req'))
- decode_out: bfloat16 [16, 2048], P('req')
Inputs may be any that keep to these rules, and one draw needn't show every extreme that they name: `prefill_routes`: each token names 6 different experts; every expert is named by some token; in each aligned block of 32 tokens no expert is named by more than 6 tokens, and in some block one expert is named by exactly 6. `decode_routes`: each decoded token names 6 different experts; every expert is named by some token. `cache_lengths`: some request has exactly 16384 cached positions.
All inputs are finite; a program needn't handle non-finite values. No bound on the sum of `cache_lengths` on one device may be relied on, other than what follows from the above.
Results may differ from a plain program's by a relative error of at most 0.02.
Values may be sent and summed in bfloat16 or wider, within the bound.
No kernel may reach another device: no remote copies, remote signals or barrier semaphores. Data moves between devices by JAX's collectives and lax.ppermute only.
A program may use at most 128 MiB of HBM per device.

v0:
```python
import jax
import jax.numpy as jnp
from jax import lax
from jax.sharding import PartitionSpec as P

NEG = -1e30
ROUTE_SCALE = 2.446


def merged(part, axis, combine):
    gathered = jax.tree.map(lambda a: lax.all_gather(a, axis), part)

    def take(source):
        return jax.tree.map(lambda a: lax.dynamic_index_in_dim(a, source, 0, False), gathered)

    return lax.fori_loop(
        1, lax.axis_size(axis), lambda source, state: combine(state, take(source)), take(0)
    )


def settle(values):
    return lax.optimization_barrier(values.astype(jnp.bfloat16)).astype(jnp.float32)


def rms_rows(rows_in, gain_row):
    widened = rows_in.astype(jnp.float32)
    mean_square = jnp.mean(widened * widened, axis=1, keepdims=True)
    return (widened * lax.rsqrt(mean_square + 1e-06) * gain_row).astype(jnp.bfloat16)


def swiglu(inputs, gate_w, up_w, down_w):
    gate_part = jnp.dot(inputs, gate_w, preferred_element_type=jnp.float32)
    up_part = jnp.dot(inputs, up_w, preferred_element_type=jnp.float32)
    hidden = (jax.nn.silu(gate_part) * up_part).astype(jnp.bfloat16)
    return jnp.dot(hidden, down_w, preferred_element_type=jnp.float32)


def gate_table(routes, scores, experts):
    shares = scores / jnp.sum(scores, axis=1, keepdims=True) * ROUTE_SCALE
    matches = routes[:, :, None] == jnp.arange(experts, dtype=jnp.int32)[None, None, :]
    return jnp.sum(jnp.where(matches, shares[:, :, None], 0.0), axis=1).astype(jnp.bfloat16)


def routed_terms(inputs, weight_rows, first_expert, gate_w, up_w, down_w):
    result = jnp.zeros(inputs.shape, jnp.float32)
    for slot_index in range(gate_w.shape[0]):
        weight_col = lax.dynamic_slice_in_dim(weight_rows, first_expert + slot_index, 1, 1).astype(
            jnp.float32
        )
        result = result + weight_col * swiglu(
            inputs, gate_w[slot_index], up_w[slot_index], down_w[slot_index]
        )
    return result


def merge_parts(first_part, second_part):
    row_peak = jnp.maximum(first_part[0], second_part[0])
    keep_first = jnp.exp(first_part[0] - row_peak)
    keep_second = jnp.exp(second_part[0] - row_peak)
    merged_total = first_part[1] * keep_first + second_part[1] * keep_second
    merged_sum = first_part[2] * keep_first[:, :, None] + second_part[2] * keep_second[:, :, None]
    return (row_peak, merged_total, merged_sum)


def local(
    prefill_resid,
    prefill_routes,
    prefill_scores,
    decode_resid,
    queries,
    latent_cache,
    new_latent,
    cache_lengths,
    decode_routes,
    decode_scores,
    norm_gain,
    absorb_key,
    absorb_value,
    out_proj,
    expert_gate,
    expert_up,
    expert_down,
    shared_gate,
    shared_up,
    shared_down,
):
    req_count = lax.axis_size("req")
    blk_count = lax.axis_size("blk")
    blk_index = lax.axis_index("blk")
    nope_width = absorb_key.shape[1]
    latent_width = absorb_key.shape[2]
    scale_factor = queries.shape[2] ** (-0.5)
    positions = latent_cache.shape[1]
    requests = queries.shape[0]
    head_count = queries.shape[1]
    q_latent = jnp.einsum(
        "ihn,hnl->ihl", queries[:, :, :nope_width], absorb_key, preferred_element_type=jnp.float32
    ).astype(jnp.bfloat16)
    q_full = jnp.concatenate([q_latent, queries[:, :, nope_width:]], axis=2)
    first_position = blk_index * positions
    live_mask = (first_position + jnp.arange(positions, dtype=jnp.int32))[None, :] < cache_lengths[
        :, None
    ]

    def local_part(operand):
        scores = (
            jnp.einsum("ihc,ipc->ihp", q_full, latent_cache, preferred_element_type=jnp.float32)
            * scale_factor
        )
        scores = jnp.where(live_mask[:, None, :], scores, NEG)
        row_peak = jnp.max(scores, axis=2)
        expo_weights = jnp.where(live_mask[:, None, :], jnp.exp(scores - row_peak[:, :, None]), 0.0)
        weighted = jnp.einsum(
            "ihp,ipl->ihl",
            expo_weights.astype(jnp.bfloat16),
            latent_cache[:, :, :latent_width],
            preferred_element_type=jnp.float32,
        )
        return (row_peak, jnp.sum(expo_weights, axis=2), weighted)

    def empty_part(operand):
        return (
            jnp.full((requests, head_count), NEG, jnp.float32),
            jnp.zeros((requests, head_count), jnp.float32),
            jnp.zeros((requests, head_count, latent_width), jnp.float32),
        )

    partials = lax.cond(jnp.max(cache_lengths) > first_position, local_part, empty_part, 0)
    row_peak, denominator, weighted = merged(partials, "blk", merge_parts)
    fresh_score = (
        jnp.einsum("ihc,ic->ih", q_full, new_latent, preferred_element_type=jnp.float32)
        * scale_factor
    )
    overall = jnp.maximum(row_peak, fresh_score)
    keep_old = jnp.exp(row_peak - overall)
    fresh_weight = jnp.exp(fresh_score - overall)
    denominator = denominator * keep_old + fresh_weight
    weighted = weighted * keep_old[:, :, None] + settle(fresh_weight)[:, :, None] * new_latent[
        :, None, :latent_width
    ].astype(jnp.float32)
    o_latent = (weighted / denominator[:, :, None]).astype(jnp.bfloat16)
    value_piece = lax.all_gather(absorb_value, "req", axis=0, tiled=True)
    proj_piece = lax.all_gather(out_proj, "req", axis=0, tiled=True)
    head_values = jnp.einsum(
        "ihl,hlv->ihv", o_latent, value_piece, preferred_element_type=jnp.float32
    ).astype(jnp.bfloat16)
    attention = jnp.einsum(
        "ihv,hvd->id", head_values, proj_piece, preferred_element_type=jnp.float32
    )
    hidden_dec = (decode_resid.astype(jnp.float32) + attention).astype(jnp.bfloat16)
    experts = expert_gate.shape[0] * blk_count
    first_expert = blk_index * expert_gate.shape[0]
    own_rows = jnp.concatenate(
        [rms_rows(prefill_resid, norm_gain), rms_rows(hidden_dec, norm_gain)], axis=0
    )
    own_table = jnp.concatenate(
        [
            gate_table(prefill_routes, prefill_scores, experts),
            gate_table(decode_routes, decode_scores, experts),
        ],
        axis=0,
    )
    tile_rows = own_rows.shape[0]
    model_width = own_rows.shape[1]
    every_rows, every_table = (
        lax.all_gather(own_rows, ("req", "blk"), axis=0, tiled=True),
        lax.all_gather(own_table, ("req", "blk"), axis=0, tiled=True),
    )
    grid_rows = every_rows.reshape(req_count, blk_count, tile_rows, model_width)
    column_rows = lax.dynamic_index_in_dim(grid_rows, blk_index, 1, keepdims=False).reshape(
        req_count * tile_rows, model_width
    )
    shared_column = swiglu(column_rows, shared_gate, shared_up, shared_down).reshape(
        req_count, tile_rows, model_width
    )
    routed = routed_terms(
        every_rows, every_table, first_expert, expert_gate, expert_up, expert_down
    )
    tile_ids = jnp.arange(tile_rows * lax.axis_size(("req", "blk")) // tile_rows, dtype=jnp.int32)
    in_column = tile_ids % blk_count == blk_index
    owner_rows = (tile_ids // blk_count)[:, None] == jnp.arange(req_count, dtype=jnp.int32)[None, :]
    selector = jnp.logical_and(in_column[:, None], owner_rows).astype(jnp.float32)
    shared_part = jnp.einsum(
        "tr,rnd->tnd", selector, shared_column, precision=lax.Precision.HIGHEST
    )
    moe_rows = lax.psum_scatter(
        routed + shared_part.reshape(tile_rows * lax.axis_size(("req", "blk")), model_width),
        ("req", "blk"),
        scatter_dimension=0,
        tiled=True,
    )
    prefill_count = prefill_resid.shape[0]
    prefill_out = (prefill_resid.astype(jnp.float32) + moe_rows[:prefill_count]).astype(
        jnp.bfloat16
    )
    decode_out = (hidden_dec.astype(jnp.float32) + moe_rows[prefill_count:]).astype(jnp.bfloat16)
    return (prefill_out, decode_out)


def solution(mesh):
    return jax.shard_map(
        local,
        mesh=mesh,
        in_specs=(
            P(("blk", "req"), None),
            P(("blk", "req"), None),
            P(("blk", "req"), None),
            P("req", None),
            P("req", None, None),
            P("req", "blk", None),
            P("req", None),
            P("req"),
            P("req", None),
            P("req", None),
            P(),
            P(),
            P("req", None, None),
            P("req", None, None),
            P("blk", None, "req"),
            P("blk", None, "req"),
            P("blk", "req", None),
            P(None, "req"),
            P(None, "req"),
            P("req", None),
        ),
        out_specs=(P(("blk", "req"), None), P("req", None)),
        check_vma=False,
    )
```

profile of v0, /device:TPU:8, one launch (start us, length us, event | category | flops | bytes accessed | tf_op | source)
XLA Modules:
  0.0 1075.9 jit_solution(22341837289912471)
XLA Ops:
  8.9 1.3 reduce_max.18
  11.3 3.6 conditional.1
  11.4 0.9 fusion.84
  13.1 1.0 fusion.1
  17.1 36.1 %all-gather.5 = f32[32,2,16]{2,1,0:T(2,128)S(1)} all-gather(f32[1,2,16]{2,1,0:T(2,128)S(1)} %bitcast.96), channel_id=3, replica_groups=mesh['req'=8,'blk'=32] {'blk'}, dimensions={0}, use_global_device_ids=true | all-gather | bytes 4224 | tf_op jit(solution)/shard_map/all_gather | solution.py:11
  53.2 30.9 %all-gather.4 = f32[32,2,16]{2,1,0:T(2,128)S(1)} all-gather(f32[1,2,16]{2,1,0:T(2,128)} %bitcast.6), channel_id=2, replica_groups=mesh['req'=8,'blk'=32] {'blk'}, dimensions={0}, use_global_device_ids=true | all-gather | bytes 4224 | tf_op jit(solution)/shard_map/all_gather | solution.py:11
  85.4 30.1 %while.19 = (s32[]{:T(128)}, f32[2,16]{1,0:T(2,128)S(1)}, f32[2,16]{1,0:T(2,128)S(1)}, f32[2,16,512]{2,1,0:T(8,128)S(1)}, f32[32,2,16]{2,1,0:T(2,128)S(1)}, /*in...) while((s32[]{:T(128)}, f32[2,16]{1,0:T(2,128)S(1)}, ...), condition=%wide.region_11.12_spmd, body=%wide.region_10.11_spmd.sunk | while | flops 49349 | bytes 198039 | solution.py:16
  86.4 0.9 fusion.104
  87.4 0.9 fusion.104
  97.1 0.9 fusion.104
  98.1 0.9 fusion.104
  103.9 0.9 fusion.104
  105.9 0.9 fusion.104
  107.8 0.9 fusion.104
  115.7 29.1 %all-gather.12.cloned.1.call-done = bf16[16,512,128]{2,1,0:T(8,128)(2,1)} async-done(((bf16[2,512,128]{2,1,0:T(8,128)(2,1)}), bf16[16,512,128]{2,1,0:T(8,128)(2,1)}) %all-gather.12.cloned.1.call-update) | async-done | bytes 2097168 | tf_op jit(solution)/shard_map/all_gather | solution.py:142
  144.8 115.6 %all-gather.14.cloned.1.call-done = bf16[16,128,2048]{2,1,0:T(8,128)(2,1)} async-done(((bf16[2,128,2048]{2,1,0:T(8,128)(2,1)}), bf16[16,128,2048]{2,1,0:T(8,128)(2,1)}) %all-gather.14.cloned.1.call-update) | async-done | bytes 8388624 | tf_op jit(solution)/shard_map/all_gather | solution.py:143
  260.4 5.6 multiply_reduce_fusion
  267.8 324.9 %all-gather.3 = bf16[256,6,64]{2,1,0:T(8,128)(2,1)S(1)} all-gather(bf16[1,6,64]{2,1,0:T(8,128)(2,1)S(1)} %maximum_bitcast_fusion.1), channel_id=1, replica_groups=mesh['req'=8,'blk'=32] {'req','blk'}, dimensions={0}, use_global_device_ids=true | all-gather | bytes 197376 | tf_op jit(solution)/shard_map/all_gather | solution.py:167
  593.5 88.7 %all-gather.18.cloned.1.call-done = bf16[256,6,2048]{2,1,0:T(8,128)(2,1)} async-done(((bf16[1,6,2048]{2,1,0:T(8,128)(2,1)}), bf16[256,6,2048]{2,1,0:T(8,128)(2,1)}) %all-gather.18.cloned.1.call-update) | async-done | bytes 6291472 | tf_op jit(solution)/shard_map/all_gather | solution.py:166
  682.1 11.0 %reshape.96 = bf16[1536,2048]{1,0:T(8,128)(2,1)} reshape(bf16[256,6,2048]{2,1,0:T(8,128)(2,1)} %all-gather.18.cloned.1.call-done) | data formatting | bytes 12582912
  693.2 6.2 fusion.36
  699.4 3.2 fusion.31
  702.6 1.1 dynamic-slice_bitcast_fusion
  704.3 2.5 fusion.21
  706.9 8.1 fusion.49
  715.0 17.8 %copy.59 = f32[256,6,2048]{2,1,0:T(8,128)} copy(f32[256,6,2048]{2,0,1:T(8,128)} %fusion.49) | data formatting | bytes 25165824 | tf_op jit(solution)/shard_map/tr,rnd->tnd/dot_general | solution.py:183
  732.8 15.9 %reshape.77 = f32[1536,2048]{1,0:T(8,128)} reshape(f32[256,6,2048]{2,1,0:T(8,128)} %copy.59) | data formatting | bytes 25165824 | tf_op jit(solution)/shard_map/reshape | solution.py:187
  748.7 11.5 %fusion.19 = f32[1536,2048]{1,0:T(8,128)} fusion(bf16[1536,2048]{1,0:T(8,128)(2,1)} %reshape.96, f32[1536,176]{0,1:T(8,128)} %fusion.36, bf16[2,176,2048]{2,1,0:T(8,128)(2,1)S(1)} %copy-done.6, bf16[2,2048,176]{1,2,0:T(8,128)(2,1)S(1)} %copy-done.7), kind=kOutput, calls=%fused_computation.32 | convolution fusion | flops 2216214528 | bytes 21397504 | tf_op jit(solution)/shard_map/dot_general | solution.py:35
  760.2 17.7 %add_add_fusion = f32[1536,2048]{1,0:T(8,128)} fusion(f32[1536,2048]{1,0:T(8,128)} %reshape.77, f32[1536,2048]{1,0:T(8,128)} %fusion.19, f32[1536]{0:T(1024)S(1)} %get-tuple-element.233, f32[1536]{0:T(1024)S(1)} %get-tuple-element.232, bf16[2,176,2048]{2,1,0:T(8,128)(2,1)S(1)} %copy-done.6, bf16[1536,2048]{1,0:T(8,128)(2,1)} %reshape.96, ...), kind=kOutput, calls=%fused_computation.23 | convolution fusion | flops 2228797440 | bytes 46579712 | tf_op jit(solution)/shard_map/dot_general | solution.py:35
  778.0 288.3 %all-reduce.3.cloned.1.call-done = f32[1536,2048]{1,0:T(8,128)} async-done(((f32[1536,2048]{1,0:T(8,128)}), f32[1536,2048]{1,0:T(8,128)}) %all-reduce.3.cloned.1.call-update) | async-done | bytes 12582928
  1066.3 1.5 fusion.62
  1067.9 1.5 fusion.65
  (148 shorter events, 33.4 us)
Async XLA Ops:
  7.2 3.7 copy-start
  7.2 4.1 copy-start.18
  7.2 4.1 copy-start.3
  7.2 77.3 %all-gather.16.cloned.1.call-start = ((), (), s32[]{:S(2)}) async-start(), calls=%async_computation.2 | async-start | bytes 2162688 | tf_op jit(solution)/shard_map/all_gather | solution.py:11
  14.9 0.6 copy-start.8
  14.9 69.3 %copy-start.16 = (bf16[2,576]{1,0:T(2,128)(2,1)S(1)}, bf16[2,576]{1,0:T(2,128)(2,1)}, u32[]{:S(2)}) copy-start(bf16[2,576]{1,0:T(2,128)(2,1)} %param.30) | copy-start | bytes 6916
  14.9 69.4 %copy-start.9 = (bf16[4,2048]{1,0:T(4,128)(2,1)S(1)}, bf16[4,2048]{1,0:T(4,128)(2,1)}, u32[]{:S(2)}) copy-start(bf16[4,2048]{1,0:T(4,128)(2,1)} %param.24) | copy-start | bytes 49156
  14.9 69.5 %copy-start.11 = (f32[2048]{0:T(1024)S(1)}, f32[2048]{0:T(1024)}, u32[]{:S(2)}) copy-start(f32[2048]{0:T(1024)} %param.34) | copy-start | bytes 24580
  15.5 129.3 %all-gather.12.cloned.1.call-start = ((), (), s32[]{:S(2)}) async-start(), calls=%async_computation | async-start | bytes 2359296 | tf_op jit(solution)/shard_map/all_gather | solution.py:142
  16.3 244.1 %copy-start.12 = (bf16[2,2048]{1,0:T(2,128)(2,1)S(1)}, bf16[2,2048]{1,0:T(2,128)(2,1)}, u32[]{:S(2)}) copy-start(bf16[2,2048]{1,0:T(2,128)(2,1)} %param.27) | copy-start | bytes 24580
  16.3 244.1 %all-gather.14.cloned.1.call-start = ((), (), s32[]{:S(2)}) async-start(), calls=%async_computation.1 | async-start | bytes 9437184 | tf_op jit(solution)/shard_map/all_gather | solution.py:143
  17.0 665.1 %all-gather.18.cloned.1.call-start = ((), (), s32[]{:S(2)}) async-start(), calls=%async_computation.3 | async-start | bytes 8421376 | tf_op jit(solution)/shard_map/all_gather | solution.py:166
  115.7 151.1 %copy-start.13 = (f32[4,6]{1,0:T(4,128)S(1)}, f32[4,6]{1,0:T(4,128)}, u32[]{:S(2)}) copy-start(f32[4,6]{1,0:T(4,128)} %param.26) | copy-start | bytes 292
  115.7 151.4 %copy-start.15 = (s32[4,6]{1,0:T(4,128)S(1)}, s32[4,6]{1,0:T(4,128)}, u32[]{:S(2)}) copy-start(s32[4,6]{1,0:T(4,128)} %param.25) | copy-start | bytes 292
  115.7 151.5 %copy-start.14 = (f32[2,6]{1,0:T(2,128)S(1)}, f32[2,6]{1,0:T(2,128)}, u32[]{:S(2)}) copy-start(f32[2,6]{1,0:T(2,128)} %param.33) | copy-start | bytes 148
  115.7 151.8 %copy-start.17 = (s32[2,6]{1,0:T(2,128)S(1)}, s32[2,6]{1,0:T(2,128)}, u32[]{:S(2)}) copy-start(s32[2,6]{1,0:T(2,128)} %param.32) | copy-start | bytes 148
  266.7 799.6 %all-reduce.3.cloned.1.call-start = ((), (), s32[]{:S(2)}) async-start(), calls=%async_computation.4 | async-start | bytes 25165824
  593.4 99.7 %copy-start.19 = (bf16[2,2048,176]{1,2,0:T(8,128)(2,1)S(1)}, bf16[2,2048,176]{1,2,0:T(8,128)(2,1)}, u32[]{:S(2)}) copy-start(bf16[2,2048,176]{1,2,0:T(8,128)(2,1)} %param.38) | copy-start | bytes 4325380
  693.2 6.2 copy-start.2
  699.4 4.4 copy-start.5
  702.6 1.7 copy-start.4
  732.8 15.9 %copy-start.6 = (bf16[2,176,2048]{2,1,0:T(8,128)(2,1)S(1)}, bf16[2,176,2048]{2,1,0:T(8,128)(2,1)}, u32[]{:S(2)}) copy-start(bf16[2,176,2048]{2,1,0:T(8,128)(2,1)} %param.40) | copy-start | bytes 4325380
  732.8 15.9 %copy-start.7 = (bf16[2,2048,176]{1,2,0:T(8,128)(2,1)S(1)}, bf16[2,2048,176]{1,2,0:T(8,128)(2,1)}, u32[]{:S(2)}) copy-start(bf16[2,2048,176]{1,2,0:T(8,128)(2,1)} %param.39) | copy-start | bytes 4325380
  777.9 288.4 %copy-start.10 = (bf16[4,2048]{1,0:T(4,128)(2,1)S(1)}, bf16[4,2048]{1,0:T(4,128)(2,1)}, u32[]{:S(2)}) copy-start(bf16[4,2048]{1,0:T(4,128)(2,1)} %param.24) | copy-start | bytes 49156
  778.0 291.4 %copy-start.1 = (bf16[16,128,512]{2,1,0:T(8,128)(2,1)S(1)}, bf16[16,128,512]{2,1,0:T(8,128)(2,1)}, u32[]{:S(2)}) copy-start(bf16[16,128,512]{2,1,0:T(8,128)(2,1)} %param.35) | copy-start | bytes 6291460
Sparse Core Ops, SparseCore 0:
  15.7 67.0 all-gather.15
  85.4 59.3 all-gather.11
  147.4 112.8 all-gather.13
  266.8 415.2 all-gather.17
  778.1 288.1 all-reduce.2
where the time goes:
time: 1080 us
  waiting for transfers between devices  523 us (48%)
  blocking collectives  392 us (36%)
  matrix products  57.8 us (5%)
  local copies, waits for them, and re-layouts  50.5 us (5%)
  other arithmetic  36.9 us (3%)
  between operations  14.8 us (1%)
    all_gather x1, blocking collectives, local(): lax.all_gather(own_table, ('req', 'blk'), axis=0, tiled=True)  325 us
    unnamed x6, waiting for transfers between devices  290 us
    all_gather x1, waiting for transfers between devices, local(): proj_piece = lax.all_gather(out_proj, 'req', axis=0, tiled=True)  116 us
    all_gather x1, waiting for transfers between devices, local(): lax.all_gather(own_rows, ('req', 'blk'), axis=0, tiled=True)  88.7 us
    all_gather x2, blocking collectives, merged(): gathered = jax.tree.map(lambda a: lax.all_gather(a, axis), part)  67.1 us
    dot_general x3, matrix products, swiglu(): return jnp.dot(hidden, down_w, preferred_element_type=jnp.float32)  31.7 us
    all_gather x1, waiting for transfers between devices, local(): value_piece = lax.all_gather(absorb_value, 'req', axis=0, tiled=True)  29.1 us
    add x31, other arithmetic, merge_parts(): first_part[2] * keep_first[:, :, None]  28.6 us
  transfers between devices with their start and end apart: 5, of which 4 were waited for; matrix products, arithmetic and copies ran while one was open for 3% of the time, Pallas kernels for 0%

commit v1 on v0

--- a/solution.py
+++ b/solution.py
@@ -5,6 +5,11 @@
 
 NEG = -1e30
 ROUTE_SCALE = 2.446
+
+
+def swapped_in(x, axis, dim):
+    outgoing = jnp.stack([x] * lax.axis_size(axis))
+    return jnp.concatenate(lax.all_to_all(outgoing, axis, 0, 0), axis=dim)
 
 
 def merged(part, axis, combine):
@@ -140,7 +145,7 @@
     ].astype(jnp.float32)
     o_latent = (weighted / denominator[:, :, None]).astype(jnp.bfloat16)
     value_piece = lax.all_gather(absorb_value, "req", axis=0, tiled=True)
-    proj_piece = lax.all_gather(out_proj, "req", axis=0, tiled=True)
+    proj_piece = swapped_in(out_proj, "req", 0)
     head_values = jnp.einsum(
         "ihl,hlv->ihv", o_latent, value_piece, preferred_element_type=jnp.float32
     ).astype(jnp.bfloat16)

time: 1080 us -> 1030 us (0.954)
  waiting for transfers between devices: 523 us -> 450 us
  blocking collectives: 392 us -> 404 us
    all_gather x1 -> x0, waiting for transfers between devices: 116 us -> none  [local(): proj_piece = lax.all_gather(out_proj, 'req', axis=0, tiled=True)]
    all_gather x1, waiting for transfers between devices: 0.02 us -> 42 us  [merged(): gathered = jax.tree.map(lambda a: lax.all_gather(a, axis), part)]
    unnamed x6 -> x5, waiting for transfers between devices: 290 us -> 290 us
  transfers between devices with their start and end apart: 5 -> 5, of which waited for: 4 -> 4; matrix products, arithmetic and copies ran while one was open for 3% -> 4% of each run, Pallas kernels for 0% -> 0%
where the time goes in v1:
time: 1030 us
  waiting for transfers between devices  450 us (44%)
  blocking collectives  404 us (39%)
  matrix products  57.8 us (6%)
  local copies, waits for them, and re-layouts  56 us (5%)
  other arithmetic  36.9 us (4%)
  between operations  14.7 us (1%)
    all_gather x1, blocking collectives, local(): lax.all_gather(own_table, ('req', 'blk'), axis=0, tiled=True)  326 us
    unnamed x5, waiting for transfers between devices  290 us
    all_gather x1, waiting for transfers between devices, local(): lax.all_gather(own_rows, ('req', 'blk'), axis=0, tiled=True)  87.8 us
    all_gather x2, blocking collectives, merged(): gathered = jax.tree.map(lambda a: lax.all_gather(a, axis), part)  77.6 us
    all_gather x1, waiting for transfers between devices, merged(): gathered = jax.tree.map(lambda a: lax.all_gather(a, axis), part)  42 us
    dot_general x3, matrix products, swiglu(): return jnp.dot(hidden, down_w, preferred_element_type=jnp.float32)  31.8 us
    all_gather x1, waiting for transfers between devices, local(): value_piece = lax.all_gather(absorb_value, 'req', axis=0, tiled=True)  30.2 us
    add x31, other arithmetic, merge_parts(): first_part[2] * keep_first[:, :, None]  28.6 us
  transfers between devices with their start and end apart: 5, of which 4 were waited for; matrix products, arithmetic and copies ran while one was open for 4% of the time, Pallas kernels for 0%

profile of v1, /device:TPU:8, one launch (start us, length us, event | category | flops | bytes accessed | tf_op | source)
XLA Modules:
  0.0 1025.2 jit_solution(18023135501450310412)
XLA Ops:
  8.9 1.3 reduce_max.18
  11.3 3.6 conditional.1
  11.4 0.9 fusion.84
  13.1 1.0 fusion.1
  15.6 5.5 stack.2
  21.1 5.1 all-to-all-start
  27.0 39.9 %all-gather.5 = f32[32,2,16]{2,1,0:T(2,128)S(1)} all-gather(f32[1,2,16]{2,1,0:T(2,128)S(1)} %bitcast.97), channel_id=3, replica_groups=mesh['req'=8,'blk'=32] {'blk'}, dimensions={0}, use_global_device_ids=true | all-gather | bytes 4224 | tf_op jit(solution)/shard_map/all_gather | solution.py:16
  66.9 37.7 %all-gather.4 = f32[32,2,16]{2,1,0:T(2,128)S(1)} all-gather(f32[1,2,16]{2,1,0:T(2,128)} %bitcast.6), channel_id=2, replica_groups=mesh['req'=8,'blk'=32] {'blk'}, dimensions={0}, use_global_device_ids=true | all-gather | bytes 4224 | tf_op jit(solution)/shard_map/all_gather | solution.py:16
  104.9 42.0 %all-gather.13.cloned.1.call-done = f32[64,16,512]{2,1,0:T(8,128)} async-done(((f32[2,16,512]{2,1,0:T(8,128)}), f32[64,16,512]{2,1,0:T(8,128)}) %all-gather.13.cloned.1.call-update) | async-done | bytes 2097168 | tf_op jit(solution)/shard_map/all_gather | solution.py:16
  147.8 30.1 %while.19 = (s32[]{:T(128)}, f32[2,16]{1,0:T(2,128)S(1)}, f32[2,16]{1,0:T(2,128)S(1)}, f32[2,16,512]{2,1,0:T(8,128)S(1)}, f32[32,2,16]{2,1,0:T(2,128)S(1)}, /*in...) while((s32[]{:T(128)}, f32[2,16]{1,0:T(2,128)S(1)}, ...), condition=%wide.region_11.12_spmd, body=%wide.region_10.11_spmd.sunk | while | flops 49349 | bytes 198039 | solution.py:21
  148.8 0.9 fusion.104
  160.5 0.9 fusion.104
  161.5 0.9 fusion.104
  169.2 0.9 fusion.104
  171.2 0.9 fusion.104
  178.1 30.2 %all-gather.11.cloned.1.call-done = bf16[16,512,128]{2,1,0:T(8,128)(2,1)} async-done(((bf16[2,512,128]{2,1,0:T(8,128)(2,1)}), bf16[16,512,128]{2,1,0:T(8,128)(2,1)}) %all-gather.11.cloned.1.call-update) | async-done | bytes 2097168 | tf_op jit(solution)/shard_map/all_gather | solution.py:147
  208.3 5.6 multiply_reduce_fusion
  215.7 326.4 %all-gather.3 = bf16[256,6,64]{2,1,0:T(8,128)(2,1)S(1)} all-gather(bf16[1,6,64]{2,1,0:T(8,128)(2,1)S(1)} %maximum_bitcast_fusion.1), channel_id=1, replica_groups=mesh['req'=8,'blk'=32] {'req','blk'}, dimensions={0}, use_global_device_ids=true | all-gather | bytes 197376 | tf_op jit(solution)/shard_map/all_gather | solution.py:172
  543.0 87.8 %all-gather.15.cloned.1.call-done = bf16[256,6,2048]{2,1,0:T(8,128)(2,1)} async-done(((bf16[1,6,2048]{2,1,0:T(8,128)(2,1)}), bf16[256,6,2048]{2,1,0:T(8,128)(2,1)}) %all-gather.15.cloned.1.call-update) | async-done | bytes 6291472 | tf_op jit(solution)/shard_map/all_gather | solution.py:171
  630.8 11.0 %reshape.102 = bf16[1536,2048]{1,0:T(8,128)(2,1)} reshape(bf16[256,6,2048]{2,1,0:T(8,128)(2,1)} %all-gather.15.cloned.1.call-done) | data formatting | bytes 12582912
  641.8 6.2 fusion.36
  648.0 3.2 fusion.31
  651.3 1.1 dynamic-slice_bitcast_fusion
  653.0 2.5 fusion.21
  655.6 8.0 fusion.49
  663.6 17.9 %copy.59 = f32[256,6,2048]{2,1,0:T(8,128)} copy(f32[256,6,2048]{2,0,1:T(8,128)} %fusion.49) | data formatting | bytes 25165824 | tf_op jit(solution)/shard_map/tr,rnd->tnd/dot_general | solution.py:188
  681.5 15.9 %reshape.83 = f32[1536,2048]{1,0:T(8,128)} reshape(f32[256,6,2048]{2,1,0:T(8,128)} %copy.59) | data formatting | bytes 25165824 | tf_op jit(solution)/shard_map/reshape | solution.py:192
  697.3 11.5 %fusion.19 = f32[1536,2048]{1,0:T(8,128)} fusion(bf16[1536,2048]{1,0:T(8,128)(2,1)} %reshape.102, f32[1536,176]{0,1:T(8,128)} %fusion.36, bf16[2,176,2048]{2,1,0:T(8,128)(2,1)S(1)} %copy-done.6, bf16[2,2048,176]{1,2,0:T(8,128)(2,1)S(1)} %copy-done.7), kind=kOutput, calls=%fused_computation.32 | convolution fusion | flops 2216214528 | bytes 21397504 | tf_op jit(solution)/shard_map/dot_general | solution.py:40
  708.8 17.8 %add_add_fusion = f32[1536,2048]{1,0:T(8,128)} fusion(f32[1536,2048]{1,0:T(8,128)} %reshape.83, f32[1536,2048]{1,0:T(8,128)} %fusion.19, f32[1536]{0:T(1024)S(1)} %get-tuple-element.233, f32[1536]{0:T(1024)S(1)} %get-tuple-element.232, bf16[2,176,2048]{2,1,0:T(8,128)(2,1)S(1)} %copy-done.6, bf16[1536,2048]{1,0:T(8,128)(2,1)} %reshape.102, ...), kind=kOutput, calls=%fused_computation.23 | convolution fusion | flops 2228797440 | bytes 46579712 | tf_op jit(solution)/shard_map/dot_general | solution.py:40
  726.6 288.9 %all-reduce.3.cloned.1.call-done = f32[1536,2048]{1,0:T(8,128)} async-done(((f32[1536,2048]{1,0:T(8,128)}), f32[1536,2048]{1,0:T(8,128)}) %all-reduce.3.cloned.1.call-update) | async-done | bytes 12582928
  1015.6 1.5 fusion.62
  1017.1 1.5 fusion.65
  (148 shorter events, 34.6 us)
Async XLA Ops:
  7.2 3.7 copy-start
  7.2 4.1 copy-start.18
  7.2 4.1 copy-start.3
  7.2 139.8 %all-gather.13.cloned.1.call-start = ((), (), s32[]{:S(2)}) async-start(), calls=%async_computation.2 | async-start | bytes 2162688 | tf_op jit(solution)/shard_map/all_gather | solution.py:16
  14.9 0.6 copy-start.8
  21.1 83.5 %copy-start.16 = (bf16[2,576]{1,0:T(2,128)(2,1)S(1)}, bf16[2,576]{1,0:T(2,128)(2,1)}, u32[]{:S(2)}) copy-start(bf16[2,576]{1,0:T(2,128)(2,1)} %param.30) | copy-start | bytes 6916
  21.1 83.6 %copy-start.9 = (bf16[4,2048]{1,0:T(4,128)(2,1)S(1)}, bf16[4,2048]{1,0:T(4,128)(2,1)}, u32[]{:S(2)}) copy-start(bf16[4,2048]{1,0:T(4,128)(2,1)} %param.24) | copy-start | bytes 49156
  21.1 83.8 %copy-start.11 = (f32[2048]{0:T(1024)S(1)}, f32[2048]{0:T(1024)}, u32[]{:S(2)}) copy-start(f32[2048]{0:T(1024)} %param.34) | copy-start | bytes 24580
  21.1 187.2 %all-to-all-start = ((bf16[8,2,128,2048]{3,2,1,0:T(8,128)(2,1)}), bf16[8,2,128,2048]{3,2,1,0:T(8,128)(2,1)}, u32[]{:S(2)}, u32[]{:S(2)}) async-start(bf16[8,2,128,2048]{3,2,1,0:T(8,128)(2,1)} %stack.2), calls=%async_computation | async-start | bytes 16777216 | tf_op jit(solution)/shard_map/all_to_all | solution.py:12
  26.2 182.1 %copy-start.12 = (bf16[2,2048]{1,0:T(2,128)(2,1)S(1)}, bf16[2,2048]{1,0:T(2,128)(2,1)}, u32[]{:S(2)}) copy-start(bf16[2,2048]{1,0:T(2,128)(2,1)} %param.27) | copy-start | bytes 24580
  26.2 182.1 %all-gather.11.cloned.1.call-start = ((), (), s32[]{:S(2)}) async-start(), calls=%async_computation.1 | async-start | bytes 2359296 | tf_op jit(solution)/shard_map/all_gather | solution.py:147
  26.9 603.8 %all-gather.15.cloned.1.call-start = ((), (), s32[]{:S(2)}) async-start(), calls=%async_computation.3 | async-start | bytes 8421376 | tf_op jit(solution)/shard_map/all_gather | solution.py:171
  208.2 6.5 copy-start.13
  208.2 6.8 copy-start.15
  208.3 6.9 copy-start.14
  208.3 7.1 copy-start.17
  214.7 800.9 %all-reduce.3.cloned.1.call-start = ((), (), s32[]{:S(2)}) async-start(), calls=%async_computation.4 | async-start | bytes 25165824
  543.0 98.8 %copy-start.19 = (bf16[2,2048,176]{1,2,0:T(8,128)(2,1)S(1)}, bf16[2,2048,176]{1,2,0:T(8,128)(2,1)}, u32[]{:S(2)}) copy-start(bf16[2,2048,176]{1,2,0:T(8,128)(2,1)} %param.38) | copy-start | bytes 4325380
  641.8 6.2 copy-start.2
  648.0 4.4 copy-start.5
  651.2 1.7 copy-start.4
  681.4 15.9 %copy-start.6 = (bf16[2,176,2048]{2,1,0:T(8,128)(2,1)S(1)}, bf16[2,176,2048]{2,1,0:T(8,128)(2,1)}, u32[]{:S(2)}) copy-start(bf16[2,176,2048]{2,1,0:T(8,128)(2,1)} %param.40) | copy-start | bytes 4325380
  681.4 15.9 %copy-start.7 = (bf16[2,2048,176]{1,2,0:T(8,128)(2,1)S(1)}, bf16[2,2048,176]{1,2,0:T(8,128)(2,1)}, u32[]{:S(2)}) copy-start(bf16[2,2048,176]{1,2,0:T(8,128)(2,1)} %param.39) | copy-start | bytes 4325380
  726.6 289.0 %copy-start.10 = (bf16[4,2048]{1,0:T(4,128)(2,1)S(1)}, bf16[4,2048]{1,0:T(4,128)(2,1)}, u32[]{:S(2)}) copy-start(bf16[4,2048]{1,0:T(4,128)(2,1)} %param.24) | copy-start | bytes 49156
  726.6 292.0 %copy-start.1 = (bf16[16,128,512]{2,1,0:T(8,128)(2,1)S(1)}, bf16[16,128,512]{2,1,0:T(8,128)(2,1)}, u32[]{:S(2)}) copy-start(bf16[16,128,512]{2,1,0:T(8,128)(2,1)} %param.35) | copy-start | bytes 6291460
Sparse Core Ops, SparseCore 0:
  15.7 131.2 all-gather.12
  149.6 58.6 all-gather.10
  214.8 415.9 all-gather.14
  726.7 288.7 all-reduce.2
